TPU v7x, 512 devices: a whole 4x8x8 slice. The times are simulated.
512 devices in a mesh: section: 16 (over x_lo, z), dp: 32 (over x_hi, y, core).
Axes of the slice: x: 4 (x_hi: 2, x_lo: 2; x = x_hi * 2 + x_lo), y: 8, z: 8, core: 2. Of those that a mesh axis runs over, the one named last changes fastest.
Arguments:
- acts_down: bfloat16 [3, 16, 32, 16, 16, 256], P(None, 'section', 'dp'), may hold values from -6 to 6
- acts_up: bfloat16 [3, 16, 32, 16, 16, 256], P(None, 'section', 'dp'), may hold values from -6 to 6
- front_down: bfloat16 [16, 32, 16, 16, 256], P('section', 'dp'), may hold values from -6 to 6
- front_up: bfloat16 [16, 32, 16, 16, 256], P('section', 'dp'), may hold values from -6 to 6
- master: float32 [16, 2304, 256], P('section', 'dp'), may hold values from -4 to 4
- moment_first: float32 [16, 2304, 256], P('section', 'dp'), may hold values from -36 to 36
- moment_second: float32 [16, 2304, 256], P('section', 'dp'), may hold values from 10 to 100
Outputs:
- dx_down: bfloat16 [3, 16, 32, 16, 16, 256], P(None, 'section', 'dp')
- dx_up: bfloat16 [3, 16, 32, 16, 16, 256], P(None, 'section', 'dp')
- new_weight: bfloat16 [16, 2304, 256], P('section', 'dp')
- new_master: float32 [16, 2304, 256], P('section', 'dp')
- new_first: float32 [16, 2304, 256], P('section', 'dp')
- new_second: float32 [16, 2304, 256], P('section', 'dp')
All inputs are finite; a program needn't handle non-finite values.
Results may differ from a plain program's by a relative error of at most 0.0025.
The roundings to bfloat16 on the way count: a program that leaves them out, or rounds other values in their place, can miss the bound.
Values may be sent and summed in bfloat16 or wider, within the bound.
No kernel may reach another device: no remote copies, remote signals or barrier semaphores. Data moves between devices by JAX's collectives and lax.ppermute only.
A program may use at most 64 MiB of HBM per device.

v0:
```python
import jax
import jax.numpy as jnp
from jax import lax
from jax.sharding import PartitionSpec as P

TICKS = 3
beta_first = 0.9
beta_second = 0.95
learn_rate = 0.01
decay_rate = 0.1
epsilon = 1e-08


def from_partner(value, axis, stride):
    return lax.ppermute(value, axis, [(i, i ^ 1 << stride) for i in range(lax.axis_size(axis))])


def passed_along(value, axis, by):
    length = lax.axis_size(axis)
    pairs = [(i, i + by) for i in range(length) if 0 <= i + by < length]
    return lax.ppermute(value, axis, pairs)


def shifted_taps(feature, direction):
    images, height, columns, channels = feature.shape
    padded = jnp.pad(feature, ((0, 0), (1, 1), (1, 1), (0, 0)))
    pieces = []
    for row_step in range(3):
        for col_step in range(3):
            row_start = 1 + direction * (row_step - 1)
            col_start = 1 + direction * (col_step - 1)
            pieces.append(
                padded[:, row_start : row_start + height, col_start : col_start + columns, :]
            )
    return jnp.concatenate(pieces, axis=3).reshape(images * height * columns, 9 * channels)


def section_front(inputs, incoming, weight):
    channels = inputs.shape[-1]
    factor = (9 * channels) ** (-0.5)
    taps_front = shifted_taps(incoming, -1).reshape(-1, 9, channels)
    kernel = weight.reshape(9, channels, channels)
    grad_hidden = lax.dot_general(
        taps_front, kernel, (((1, 2), (0, 2)), ((), ())), preferred_element_type=jnp.float32
    )
    grad_hidden = factor * grad_hidden.reshape(inputs.shape)
    widened = inputs.astype(jnp.float32)
    hidden, pullback = jax.vjp(jax.nn.gelu, widened)
    outgoing = (incoming.astype(jnp.float32) + pullback(grad_hidden)[0]).astype(jnp.bfloat16)
    return (outgoing, hidden.astype(jnp.bfloat16))


def weight_term(hiddens, seen):
    channels = hiddens[0].shape[-1]
    factor = (9 * channels) ** (-0.5)
    summed = jnp.zeros((9 * channels, channels), jnp.float32)
    for hidden, incoming in zip(hiddens, seen):
        taps_hidden = shifted_taps(hidden, 1)
        summed = summed + lax.dot_general(
            taps_hidden,
            incoming.reshape(-1, channels),
            (((0,), (0,)), ((), ())),
            preferred_element_type=jnp.float32,
        )
    return factor * summed


def per_device(acts_down, acts_up, front_down, front_up, master, moment_first, moment_second):
    sections = lax.axis_size("section")
    own_rows = master[0].astype(jnp.bfloat16)
    mirror_rows = own_rows
    for bit_number in range(sections.bit_length() - 1):
        mirror_rows = from_partner(mirror_rows, "section", bit_number)
    own_weight, mirror_weight = (
        lax.all_gather(own_rows, "dp", axis=0, tiled=True),
        lax.all_gather(mirror_rows, "dp", axis=0, tiled=True),
    )
    grad_down = front_down[0]
    grad_up = front_up[0]
    seen_down = []
    seen_up = []
    hidden_down = []
    hidden_up = []
    outs_down = []
    outs_up = []
    for tick_index in range(TICKS):
        seen_down.append(grad_down)
        seen_up.append(grad_up)
        next_down, hid_down = section_front(acts_down[tick_index, 0], grad_down, own_weight)
        next_up, hid_up = section_front(acts_up[tick_index, 0], grad_up, mirror_weight)
        hidden_down.append(hid_down)
        hidden_up.append(hid_up)
        outs_down.append(next_down)
        outs_up.append(next_up)
        if tick_index + 1 < TICKS:
            grad_down = passed_along(next_down, "section", -1)
            grad_up = passed_along(next_up, "section", 1)
    term_down = weight_term(hidden_down, seen_down)
    term_up = weight_term(hidden_up, seen_up)
    full_down, full_up = (
        lax.psum(term_down.astype(jnp.bfloat16), "dp").astype(jnp.float32),
        lax.psum(term_up.astype(jnp.bfloat16), "dp").astype(jnp.float32),
    )
    shard_rows = term_down.shape[0] // lax.axis_size("dp")
    row_start = lax.axis_index("dp") * shard_rows
    down_rows = lax.dynamic_slice_in_dim(full_down, row_start, shard_rows, 0)
    up_rows = lax.dynamic_slice_in_dim(full_up, row_start, shard_rows, 0)
    mirror_grad = up_rows
    for bit_number in range(sections.bit_length() - 1):
        mirror_grad = from_partner(mirror_grad.astype(jnp.bfloat16), "section", bit_number).astype(
            mirror_grad.dtype
        )
    gradient = down_rows + mirror_grad
    old_master = master[0]
    new_first = beta_first * moment_first[0] + (1.0 - beta_first) * gradient
    new_second = beta_second * moment_second[0] + (1.0 - beta_second) * gradient * gradient
    new_master = old_master - learn_rate * (
        new_first / (jnp.sqrt(new_second) + epsilon) + decay_rate * old_master
    )
    return (
        jnp.stack(outs_down)[:, None],
        jnp.stack(outs_up)[:, None],
        new_master.astype(jnp.bfloat16)[None],
        new_master[None],
        new_first[None],
        new_second[None],
    )


def solution(mesh):
    placed = (
        P(None, "section", "dp", None, None, None),
        P(None, "section", "dp", None, None, None),
        P("section", "dp", None, None, None),
        P("section", "dp", None, None, None),
        P("section", "dp", None),
        P("section", "dp", None),
        P("section", "dp", None),
    )
    return jax.shard_map(
        per_device,
        mesh=mesh,
        in_specs=placed,
        out_specs=(
            P(None, "section", "dp", None, None, None),
            P(None, "section", "dp", None, None, None),
            P("section", "dp", None),
            P("section", "dp", None),
            P("section", "dp", None),
            P("section", "dp", None),
        ),
        check_vma=False,
    )
```

profile of v0, /device:TPU:2, one launch (start us, length us, event | category | flops | bytes accessed | tf_op | source)
XLA Modules:
  0.0 534.1 jit_solution(15789119350843120180)
XLA Ops:
  8.8 4.3 collective-permute-start.2
  32.8 6.1 %collective-permute-start.3 = (bf16[72,256]{1,0:T(8,128)(2,1)S(1)}, bf16[72,256]{1,0:T(8,128)(2,1)S(1)}, u32[]{:S(2)}, u32[]{:S(2)}) collective-permute-start(bf16[72,256]{1,0:T(8,128)(2,1)S(1)} %collective-permute-done.2), channel_id=1, source_target_pairs={{0,64},{32,96},{64,0},{96,32},{128,192},{160,224},{192,128},{224,1... | collective-permute-start | bytes 110600 | tf_op jit(solution)/shard_map/ppermute | solution.py:15
  40.8 9.1 %collective-permute-start.4 = (bf16[72,256]{1,0:T(8,128)(2,1)S(1)}, bf16[72,256]{1,0:T(8,128)(2,1)S(1)}, u32[]{:S(2)}, u32[]{:S(2)}) collective-permute-start(bf16[72,256]{1,0:T(8,128)(2,1)S(1)} %collective-permute-done.3), channel_id=1, source_target_pairs={{0,128},{32,160},{64,192},{96,224},{128,0},{160,32},{192,64},{224,... | collective-permute-start | bytes 110600 | tf_op jit(solution)/shard_map/ppermute | solution.py:15
  55.4 3.5 dot_general.48
  60.3 3.3 fusion.219
  63.5 35.4 %all-gather.3.cloned.1.call-done = bf16[2304,256]{1,0:T(8,128)(2,1)} async-done(((bf16[72,256]{1,0:T(8,128)(2,1)}), bf16[2304,256]{1,0:T(8,128)(2,1)}) %all-gather.3.cloned.1.call-update) | async-done | bytes 1179664 | tf_op jit(solution)/shard_map/all_gather | solution.py:75
  98.9 2.9 fusion.119
  101.8 6.8 %collective-permute-start = (bf16[1,16,16,256]{3,2,1,0:T(8,128)(2,1)S(1)}, bf16[1,16,16,256]{3,2,1,0:T(8,128)(2,1)S(1)}, u32[]{:S(2)}, u32[]{:S(2)}) collective-permute-start(bf16[1,16,16,256]{3,2,1,0:T(8,128)(2,1)S(1)} %bitcast.548), channel_id=1, source_target_pairs={{32,0},{64,32},{96,64},{128,96},{160,128},{192,160},{224,192},{256... | collective-permute-start | bytes 393224 | tf_op jit(solution)/shard_map/ppermute | solution.py:21
  109.2 3.6 dot_general.54
  119.9 3.5 dot_general.50
  123.4 3.5 fusion.125
  126.9 4.6 collective-permute-start.1
  131.6 51.5 %all-gather.5.cloned.1.call-done = bf16[2304,256]{1,0:T(8,128)(2,1)} async-done(((bf16[72,256]{1,0:T(8,128)(2,1)}), bf16[2304,256]{1,0:T(8,128)(2,1)}) %all-gather.5.cloned.1.call-update) | async-done | bytes 1179664 | tf_op jit(solution)/shard_map/all_gather | solution.py:76
  183.1 3.0 fusion.139
  186.1 3.7 collective-permute-start.6
  191.8 4.9 collective-permute-done.6
  203.0 3.5 dot_general.56
  206.5 3.0 fusion.145
  211.7 3.7 fusion.7
  215.3 3.4 collective-permute-done.7
  238.7 256.8 %all-reduce.15.cloned.1.call-done = (bf16[2304,256]{1,0:T(8,128)(2,1)}, bf16[2304,256]{1,0:T(8,128)(2,1)}) async-done(((bf16[2304,256]{1,0:T(8,128)(2,1)}, bf16[2304,256]{1,0:T(8,128)(2,1)}), (bf16[2304,256]{1,0:T(8,128)(2,1)}, bf16[2304,256]{1,0:T(8,128)(2,1)})) %all-reduce.15.cloned.1.call-update) | async-done | bytes 2359312 | tf_op jit(solution)/shard_map/psum | solution.py:102
  496.2 3.5 collective-permute-start.8
  502.0 4.6 collective-permute-start.9
  509.9 7.3 %collective-permute-start.10 = (bf16[72,256]{1,0:T(8,128)(2,1)S(1)}, bf16[72,256]{1,0:T(8,128)(2,1)S(1)}, u32[]{:S(2)}, u32[]{:S(2)}) collective-permute-start(bf16[72,256]{1,0:T(8,128)(2,1)S(1)} %collective-permute-done.9), channel_id=1, source_target_pairs={{0,128},{32,160},{64,192},{96,224},{128,0},{160,32},{192,64},{224,... | collective-permute-start | bytes 110600 | tf_op jit(solution)/shard_map/ppermute | solution.py:15
  (178 shorter events, 84.0 us)
Async XLA Ops:
  7.2 9.8 %copy-start = (bf16[1,1,16,16,256]{4,3,2,1,0:T(8,128)(2,1)S(1)}, bf16[1,1,16,16,256]{4,3,2,1,0:T(8,128)(2,1)}, u32[]{:S(2)}) copy-start(bf16[1,1,16,16,256]{4,3,2,1,0:T(8,128)(2,1)} %param.9) | copy-start | bytes 393220
  7.2 91.8 %all-gather.3.cloned.1.call-start = ((), (), s32[]{:S(2)}) async-start(), calls=%async_computation | async-start | bytes 1216512 | tf_op jit(solution)/shard_map/all_gather | solution.py:75
  8.8 174.3 %all-gather.5.cloned.1.call-start = ((), (), s32[]{:S(2)}) async-start(), calls=%async_computation.1 | async-start | bytes 1216512 | tf_op jit(solution)/shard_map/all_gather | solution.py:76
  8.8 23.9 %collective-permute-start.2 = (bf16[72,256]{1,0:T(8,128)(2,1)}, bf16[72,256]{1,0:T(8,128)(2,1)S(1)}, u32[]{:S(2)}, u32[]{:S(2)}) collective-permute-start(bf16[72,256]{1,0:T(8,128)(2,1)} %bitcast_convert_fusion), channel_id=1, source_target_pairs={{0,32},{32,0},{64,96},{96,64},{128,160},{160,128},{192,224},{224,1... | collective-permute-start | bytes 110600 | tf_op jit(solution)/shard_map/ppermute | solution.py:15
  32.7 17.9 %copy-start.17 = (bf16[1,16,16,2304]{3,2,1,0:T(8,128)(2,1)}, bf16[1,16,16,2304]{3,2,1,0:T(8,128)(2,1)S(1)}, u32[]{:S(2)}) copy-start(bf16[1,16,16,2304]{3,2,1,0:T(8,128)(2,1)S(1)} %constant_dynamic-update-slice_fusion.72) | copy-start | bytes 3538948
  32.8 8.0 %collective-permute-start.3 = (bf16[72,256]{1,0:T(8,128)(2,1)S(1)}, bf16[72,256]{1,0:T(8,128)(2,1)S(1)}, u32[]{:S(2)}, u32[]{:S(2)}) collective-permute-start(bf16[72,256]{1,0:T(8,128)(2,1)S(1)} %collective-permute-done.2), channel_id=1, source_target_pairs={{0,64},{32,96},{64,0},{96,32},{128,192},{160,224},{192,128},{224,1... | collective-permute-start | bytes 110600 | tf_op jit(solution)/shard_map/ppermute | solution.py:15
  40.8 11.1 %collective-permute-start.4 = (bf16[72,256]{1,0:T(8,128)(2,1)S(1)}, bf16[72,256]{1,0:T(8,128)(2,1)S(1)}, u32[]{:S(2)}, u32[]{:S(2)}) collective-permute-start(bf16[72,256]{1,0:T(8,128)(2,1)S(1)} %collective-permute-done.3), channel_id=1, source_target_pairs={{0,128},{32,160},{64,192},{96,224},{128,0},{160,32},{192,64},{224,... | collective-permute-start | bytes 110600 | tf_op jit(solution)/shard_map/ppermute | solution.py:15
  51.9 7.0 %collective-permute-start.5 = (bf16[72,256]{1,0:T(8,128)(2,1)S(1)}, bf16[72,256]{1,0:T(8,128)(2,1)S(1)}, u32[]{:S(2)}, u32[]{:S(2)}) collective-permute-start(bf16[72,256]{1,0:T(8,128)(2,1)S(1)} %collective-permute-done.4), channel_id=1, source_target_pairs={{0,256},{32,288},{64,320},{96,352},{128,384},{160,416},{192,448},{... | collective-permute-start | bytes 110600 | tf_op jit(solution)/shard_map/ppermute | solution.py:15
  59.5 435.9 %all-reduce.15.cloned.1.call-start = ((), (), s32[]{:S(2)}) async-start(), calls=%async_computation.2 | async-start | bytes 4718592 | tf_op jit(solution)/shard_map/psum | solution.py:102
  101.8 11.7 %collective-permute-start = (bf16[1,16,16,256]{3,2,1,0:T(8,128)(2,1)S(1)}, bf16[1,16,16,256]{3,2,1,0:T(8,128)(2,1)S(1)}, u32[]{:S(2)}, u32[]{:S(2)}) collective-permute-start(bf16[1,16,16,256]{3,2,1,0:T(8,128)(2,1)S(1)} %bitcast.548), channel_id=1, source_target_pairs={{32,0},{64,32},{96,64},{128,96},{160,128},{192,160},{224,192},{256... | collective-permute-start | bytes 393224 | tf_op jit(solution)/shard_map/ppermute | solution.py:21
  126.9 62.9 %collective-permute-start.1 = (bf16[1,16,16,256]{3,2,1,0:T(8,128)(2,1)}, bf16[1,16,16,256]{3,2,1,0:T(8,128)(2,1)S(1)}, u32[]{:S(2)}, u32[]{:S(2)}) collective-permute-start(bf16[1,16,16,256]{3,2,1,0:T(8,128)(2,1)} %fusion.125), channel_id=1, source_target_pairs={{32,0},{64,32},{96,64},{128,96},{160,128},{192,160},{224,192},{256... | collective-permute-start | bytes 393224 | tf_op jit(solution)/shard_map/ppermute | solution.py:21
  183.1 6.8 %copy-start.18 = (bf16[1,16,16,2304]{3,2,1,0:T(8,128)(2,1)S(1)}, bf16[1,16,16,2304]{3,2,1,0:T(8,128)(2,1)}, u32[]{:S(2)}) copy-start(bf16[1,16,16,2304]{3,2,1,0:T(8,128)(2,1)} %copy-done.17) | copy-start | bytes 3538948
  186.1 10.6 %collective-permute-start.6 = (bf16[1,16,16,256]{3,2,1,0:T(8,128)(2,1)S(1)}, bf16[1,16,16,256]{3,2,1,0:T(8,128)(2,1)S(1)}, u32[]{:S(2)}, u32[]{:S(2)}) collective-permute-start(bf16[1,16,16,256]{3,2,1,0:T(8,128)(2,1)S(1)} %bitcast.546), channel_id=1, source_target_pairs={{0,32},{32,64},{64,96},{96,128},{128,160},{160,192},{192,224},{224... | collective-permute-start | bytes 393224 | tf_op jit(solution)/shard_map/ppermute | solution.py:21
  209.6 5.8 %copy-start.8 = (bf16[1,16,16,256]{3,2,1,0:T(8,128)(2,1)}, bf16[1,16,16,256]{3,2,1,0:T(8,128)(2,1)S(1)}, u32[]{:S(2)}) copy-start(bf16[1,16,16,256]{3,2,1,0:T(8,128)(2,1)S(1)} %fusion.145) | copy-start | bytes 393220
  209.6 9.2 %copy-start.16 = (bf16[1,16,16,2304]{3,2,1,0:T(8,128)(2,1)S(1)}, bf16[1,16,16,2304]{3,2,1,0:T(8,128)(2,1)}, u32[]{:S(2)}) copy-start(bf16[1,16,16,2304]{3,2,1,0:T(8,128)(2,1)} %copy-done.15) | copy-start | bytes 3538948
  209.6 9.2 %collective-permute-start.7 = (bf16[1,16,16,256]{3,2,1,0:T(8,128)(2,1)S(1)}, bf16[1,16,16,256]{3,2,1,0:T(8,128)(2,1)S(1)}, u32[]{:S(2)}, u32[]{:S(2)}) collective-permute-start(bf16[1,16,16,256]{3,2,1,0:T(8,128)(2,1)S(1)} %fusion.145), channel_id=1, source_target_pairs={{0,32},{32,64},{64,96},{96,128},{128,160},{160,192},{192,224},{224... | collective-permute-start | bytes 393224 | tf_op jit(solution)/shard_map/ppermute | solution.py:21
  496.2 5.8 %collective-permute-start.8 = (bf16[72,256]{1,0:T(8,128)(2,1)S(1)}, bf16[72,256]{1,0:T(8,128)(2,1)S(1)}, u32[]{:S(2)}, u32[]{:S(2)}) collective-permute-start(bf16[72,256]{1,0:T(8,128)(2,1)S(1)} %convert_convert_fusion), channel_id=1, source_target_pairs={{0,32},{32,0},{64,96},{96,64},{128,160},{160,128},{192,224},{224,1... | collective-permute-start | bytes 110600 | tf_op jit(solution)/shard_map/ppermute | solution.py:15
  502.0 7.8 %collective-permute-start.9 = (bf16[72,256]{1,0:T(8,128)(2,1)S(1)}, bf16[72,256]{1,0:T(8,128)(2,1)S(1)}, u32[]{:S(2)}, u32[]{:S(2)}) collective-permute-start(bf16[72,256]{1,0:T(8,128)(2,1)S(1)} %collective-permute-done.8), channel_id=1, source_target_pairs={{0,64},{32,96},{64,0},{96,32},{128,192},{160,224},{192,128},{224,1... | collective-permute-start | bytes 110600 | tf_op jit(solution)/shard_map/ppermute | solution.py:15
  509.8 12.6 %copy-start.9 = (bf16[1,16,16,256]{3,2,1,0:T(8,128)(2,1)S(1)}, bf16[1,16,16,256]{3,2,1,0:T(8,128)(2,1)}, u32[]{:S(2)}) copy-start(bf16[1,16,16,256]{3,2,1,0:T(8,128)(2,1)} %copy-done.8) | copy-start | bytes 393220
  509.8 16.2 %copy-start.7 = (f32[1,72,256]{2,1,0:T(8,128)S(1)}, f32[1,72,256]{2,1,0:T(8,128)}, u32[]{:S(2)}) copy-start(f32[1,72,256]{2,1,0:T(8,128)} %param.11) | copy-start | bytes 221188
  509.9 16.2 %copy-start.10 = (f32[1,72,256]{2,1,0:T(8,128)S(1)}, f32[1,72,256]{2,1,0:T(8,128)}, u32[]{:S(2)}) copy-start(f32[1,72,256]{2,1,0:T(8,128)} %param.13) | copy-start | bytes 221188
  509.9 16.2 %copy-start.11 = (f32[1,72,256]{2,1,0:T(8,128)S(1)}, f32[1,72,256]{2,1,0:T(8,128)}, u32[]{:S(2)}) copy-start(f32[1,72,256]{2,1,0:T(8,128)} %param.12) | copy-start | bytes 221188
  509.9 10.3 %collective-permute-start.10 = (bf16[72,256]{1,0:T(8,128)(2,1)S(1)}, bf16[72,256]{1,0:T(8,128)(2,1)S(1)}, u32[]{:S(2)}, u32[]{:S(2)}) collective-permute-start(bf16[72,256]{1,0:T(8,128)(2,1)S(1)} %collective-permute-done.9), channel_id=1, source_target_pairs={{0,128},{32,160},{64,192},{96,224},{128,0},{160,32},{192,64},{224,... | collective-permute-start | bytes 110600 | tf_op jit(solution)/shard_map/ppermute | solution.py:15
  520.2 5.8 %collective-permute-start.11 = (bf16[72,256]{1,0:T(8,128)(2,1)S(1)}, bf16[72,256]{1,0:T(8,128)(2,1)S(1)}, u32[]{:S(2)}, u32[]{:S(2)}) collective-permute-start(bf16[72,256]{1,0:T(8,128)(2,1)S(1)} %collective-permute-done.10), channel_id=1, source_target_pairs={{0,256},{32,288},{64,320},{96,352},{128,384},{160,416},{192,448},{... | collective-permute-start | bytes 110600 | tf_op jit(solution)/shard_map/ppermute | solution.py:15
  (10 other events, 23.1 us)
Sparse Core Ops, SparseCore 0:
  11.8 87.0 all-gather.2
  102.8 80.2 all-gather.4
  221.1 274.2 all-reduce.14
where the time goes:
time: 535 us; the launch traced here: 534 us
  waiting for transfers between devices  360 us (67%)
  local copies, waits for them, and re-layouts  65.3 us (12%)
  starting transfers between devices  57.3 us (11%)
  matrix products  28.5 us (5%)
  between operations  14.5 us (3%)
  other arithmetic  8.8 us (2%)
    psum x1, waiting for transfers between devices, per_device(): lax.psum(term_up.astype(jnp.bfloat16), 'dp').astype(jnp.float32)  257 us
    all_gather x1, waiting for transfers between devices, per_device(): lax.all_gather(mirror_rows, 'dp', axis=0, tiled=True)  51.5 us
    unnamed x126, local copies, waits for them, and re-layouts  40.9 us
    ppermute x8, starting transfers between devices, from_partner(): lax.ppermute(value, axis, [(i, i ^ 1 << stride) for i in range(lax.axis_s...  40 us
    all_gather x1, waiting for transfers between devices, per_device(): lax.all_gather(own_rows, 'dp', axis=0, tiled=True)  35.4 us
    dot_general x6, local copies, waits for them, and re-layouts, section_front(): lax.dot_general(taps_front, kernel, (((1, 2), (0, 2)), ((), ())), preferr...  19.1 us
    ppermute x4, starting transfers between devices, passed_along(): return lax.ppermute(value, axis, pairs)  17.2 us
    dot_general x6, matrix products, section_front(): lax.dot_general(taps_front, kernel, (((1, 2), (0, 2)), ((), ())), preferr...  16.9 us
  transfers between devices with their start and end apart: 15, of which 10 were waited for; matrix products, arithmetic and copies ran while one was open for 15% of the time, Pallas kernels for 0%

commit v1 on v0

--- a/solution.py
+++ b/solution.py
@@ -73,7 +73,9 @@
         mirror_rows = from_partner(mirror_rows, "section", bit_number)
     own_weight, mirror_weight = (
         lax.all_gather(own_rows, "dp", axis=0, tiled=True),
-        lax.all_gather(mirror_rows, "dp", axis=0, tiled=True),
+        jnp.concatenate(
+            lax.all_to_all(jnp.stack([mirror_rows] * lax.axis_size("dp")), "dp", 0, 0), axis=0
+        ),
     )
     grad_down = front_down[0]
     grad_up = front_up[0]

time: 535 us -> 482 us (0.901)
  waiting for transfers between devices: 360 us -> 293 us
  local copies, waits for them, and re-layouts: 65.3 us -> 73.6 us
    all_gather x1 -> x0, waiting for transfers between devices: 51.5 us -> none  [per_device(): lax.all_gather(mirror_rows, 'dp', axis=0, tiled=True)]
    all_gather x1, waiting for transfers between devices: 35.4 us -> 22.5 us  [per_device(): lax.all_gather(own_rows, 'dp', axis=0, tiled=True)]
    all_to_all x0 -> x1, starting transfers between devices: none -> 9.08 us  [per_device(): lax.all_to_all(jnp.stack([mirror_rows] * lax.axis_size('dp')), 'dp', 0, 0)]
    unnamed x126 -> x122, local copies, waits for them, and re-layouts: 40.9 us -> 46 us
  transfers between devices with their start and end apart: 15 -> 15, of which waited for: 10 -> 9; matrix products, arithmetic and copies ran while one was open for 15% -> 19% of each run, Pallas kernels for 0% -> 0%
where the time goes in v1:
time: 482 us; the launch traced here: 481 us
  waiting for transfers between devices  293 us (61%)
  local copies, waits for them, and re-layouts  73.6 us (15%)
  starting transfers between devices  61.9 us (13%)
  matrix products  29 us (6%)
  between operations  14.7 us (3%)
  other arithmetic  8.58 us (2%)
    psum x1, waiting for transfers between devices, per_device(): lax.psum(term_up.astype(jnp.bfloat16), 'dp').astype(jnp.float32)  255 us
    unnamed x122, local copies, waits for them, and re-layouts  46 us
    ppermute x8, starting transfers between devices, from_partner(): lax.ppermute(value, axis, [(i, i ^ 1 << stride) for i in range(lax.axis_s...  40 us
    all_gather x1, waiting for transfers between devices, per_device(): lax.all_gather(own_rows, 'dp', axis=0, tiled=True)  22.5 us
    dot_general x6, local copies, waits for them, and re-layouts, section_front(): lax.dot_general(taps_front, kernel, (((1, 2), (0, 2)), ((), ())), preferr...  19.1 us
    dot_general x6, matrix products, section_front(): lax.dot_general(taps_front, kernel, (((1, 2), (0, 2)), ((), ())), preferr...  16.2 us
    ppermute x4, starting transfers between devices, passed_along(): return lax.ppermute(value, axis, pairs)  12.8 us
    dot_general x6, matrix products, weight_term(): lax.dot_general(taps_hidden, incoming.reshape(-1, channels), (((0,), (0,)...  12.8 us
  transfers between devices with their start and end apart: 15, of which 9 were waited for; matrix products, arithmetic and copies ran while one was open for 19% of the time, Pallas kernels for 0%

profile of v1, /device:TPU:2, one launch (start us, length us, event | category | flops | bytes accessed | tf_op | source)
XLA Modules:
  0.0 481.2 jit_solution(16130331217690836442)
XLA Ops:
  8.8 4.3 collective-permute-start.2
  41.0 6.1 %collective-permute-start.3 = (bf16[72,256]{1,0:T(8,128)(2,1)S(1)}, bf16[72,256]{1,0:T(8,128)(2,1)S(1)}, u32[]{:S(2)}, u32[]{:S(2)}) collective-permute-start(bf16[72,256]{1,0:T(8,128)(2,1)S(1)} %collective-permute-done.2), channel_id=1, source_target_pairs={{0,64},{32,96},{64,0},{96,32},{128,192},{160,224},{192,128},{224,1... | collective-permute-start | bytes 110600 | tf_op jit(solution)/shard_map/ppermute | solution.py:15
  49.0 9.1 %collective-permute-start.4 = (bf16[72,256]{1,0:T(8,128)(2,1)S(1)}, bf16[72,256]{1,0:T(8,128)(2,1)S(1)}, u32[]{:S(2)}, u32[]{:S(2)}) collective-permute-start(bf16[72,256]{1,0:T(8,128)(2,1)S(1)} %collective-permute-done.3), channel_id=1, source_target_pairs={{0,128},{32,160},{64,192},{96,224},{128,0},{160,32},{192,64},{224,... | collective-permute-start | bytes 110600 | tf_op jit(solution)/shard_map/ppermute | solution.py:15
  63.6 3.6 dot_general.48
  68.3 9.1 %all-to-all-start = ((bf16[32,72,256]{2,1,0:T(8,128)(2,1)}), bf16[32,72,256]{2,1,0:T(8,128)(2,1)}, u32[]{:S(2)}, u32[]{:S(2)}) async-start(bf16[32,72,256]{2,1,0:T(8,128)(2,1)} %stack.22), calls=%async_computation | async-start | bytes 2359296 | tf_op jit(solution)/shard_map/all_to_all | solution.py:77
  78.1 3.2 fusion.219
  81.4 22.5 %all-gather.2.cloned.1.call-done = bf16[2304,256]{1,0:T(8,128)(2,1)} async-done(((bf16[72,256]{1,0:T(8,128)(2,1)}), bf16[2304,256]{1,0:T(8,128)(2,1)}) %all-gather.2.cloned.1.call-update) | async-done | bytes 1179664 | tf_op jit(solution)/shard_map/all_gather | solution.py:75
  103.9 2.9 fusion.119
  106.8 4.0 collective-permute-start
  111.5 3.6 dot_general.54
  122.0 3.6 dot_general.50
  125.6 2.9 fusion.125
  128.4 4.6 collective-permute-start.1
  133.1 3.0 fusion.139
  140.2 4.9 %collective-permute-done.6 = bf16[1,16,16,256]{3,2,1,0:T(8,128)(2,1)S(1)} collective-permute-done((bf16[1,16,16,256]{3,2,1,0:T(8,128)(2,1)S(1)}, bf16[1,16,16,256]{3,2,1,0:T(8,128)(2,1)S(1)}, u32[]{:S(2)}, u32[]{:S(2)}) %collective-permute-start.6) | collective-permute-done | bytes 131104 | tf_op jit(solution)/shard_map/ppermute | solution.py:21
  151.4 3.6 dot_general.56
  154.9 3.0 fusion.145
  160.1 3.7 fusion.7
  163.7 3.4 collective-permute-done.7
  167.6 2.9 fusion.6
  187.4 254.8 %all-reduce.15.cloned.1.call-done = (bf16[2304,256]{1,0:T(8,128)(2,1)}, bf16[2304,256]{1,0:T(8,128)(2,1)}) async-done(((bf16[2304,256]{1,0:T(8,128)(2,1)}, bf16[2304,256]{1,0:T(8,128)(2,1)}), (bf16[2304,256]{1,0:T(8,128)(2,1)}, bf16[2304,256]{1,0:T(8,128)(2,1)})) %all-reduce.15.cloned.1.call-update) | async-done | bytes 2359312 | tf_op jit(solution)/shard_map/psum | solution.py:104
  443.0 3.5 collective-permute-start.8
  448.8 4.6 collective-permute-start.9
  456.7 7.3 %collective-permute-start.10 = (bf16[72,256]{1,0:T(8,128)(2,1)S(1)}, bf16[72,256]{1,0:T(8,128)(2,1)S(1)}, u32[]{:S(2)}, u32[]{:S(2)}) collective-permute-start(bf16[72,256]{1,0:T(8,128)(2,1)S(1)} %collective-permute-done.9), channel_id=1, source_target_pairs={{0,128},{32,160},{64,192},{96,224},{128,0},{160,32},{192,64},{224,... | collective-permute-start | bytes 110600 | tf_op jit(solution)/shard_map/ppermute | solution.py:15
  (174 shorter events, 92.4 us)
Async XLA Ops:
  7.2 9.7 %copy-start = (bf16[1,1,16,16,256]{4,3,2,1,0:T(8,128)(2,1)S(1)}, bf16[1,1,16,16,256]{4,3,2,1,0:T(8,128)(2,1)}, u32[]{:S(2)}) copy-start(bf16[1,1,16,16,256]{4,3,2,1,0:T(8,128)(2,1)} %param.9) | copy-start | bytes 393220
  7.2 96.7 %all-gather.2.cloned.1.call-start = ((), (), s32[]{:S(2)}) async-start(), calls=%async_computation.1 | async-start | bytes 1216512 | tf_op jit(solution)/shard_map/all_gather | solution.py:75
  8.8 32.2 %collective-permute-start.2 = (bf16[72,256]{1,0:T(8,128)(2,1)}, bf16[72,256]{1,0:T(8,128)(2,1)S(1)}, u32[]{:S(2)}, u32[]{:S(2)}) collective-permute-start(bf16[72,256]{1,0:T(8,128)(2,1)} %bitcast_convert_fusion), channel_id=1, source_target_pairs={{0,32},{32,0},{64,96},{96,64},{128,160},{160,128},{192,224},{224,1... | collective-permute-start | bytes 110600 | tf_op jit(solution)/shard_map/ppermute | solution.py:15
  17.1 6.3 %copy-start.4 = (bf16[3,1,1,16,16,256]{5,4,3,2,1,0:T(8,128)(2,1)S(1)}, bf16[3,1,1,16,16,256]{5,4,3,2,1,0:T(8,128)(2,1)}, u32[]{:S(2)}) copy-start(bf16[3,1,1,16,16,256]{5,4,3,2,1,0:T(8,128)(2,1)} %param.8) | copy-start | bytes 1179652
  41.0 17.9 %copy-start.15 = (bf16[1,16,16,2304]{3,2,1,0:T(8,128)(2,1)}, bf16[1,16,16,2304]{3,2,1,0:T(8,128)(2,1)S(1)}, u32[]{:S(2)}) copy-start(bf16[1,16,16,2304]{3,2,1,0:T(8,128)(2,1)S(1)} %constant_dynamic-update-slice_fusion.72) | copy-start | bytes 3538948
  41.0 8.0 %collective-permute-start.3 = (bf16[72,256]{1,0:T(8,128)(2,1)S(1)}, bf16[72,256]{1,0:T(8,128)(2,1)S(1)}, u32[]{:S(2)}, u32[]{:S(2)}) collective-permute-start(bf16[72,256]{1,0:T(8,128)(2,1)S(1)} %collective-permute-done.2), channel_id=1, source_target_pairs={{0,64},{32,96},{64,0},{96,32},{128,192},{160,224},{192,128},{224,1... | collective-permute-start | bytes 110600 | tf_op jit(solution)/shard_map/ppermute | solution.py:15
  49.0 11.1 %collective-permute-start.4 = (bf16[72,256]{1,0:T(8,128)(2,1)S(1)}, bf16[72,256]{1,0:T(8,128)(2,1)S(1)}, u32[]{:S(2)}, u32[]{:S(2)}) collective-permute-start(bf16[72,256]{1,0:T(8,128)(2,1)S(1)} %collective-permute-done.3), channel_id=1, source_target_pairs={{0,128},{32,160},{64,192},{96,224},{128,0},{160,32},{192,64},{224,... | collective-permute-start | bytes 110600 | tf_op jit(solution)/shard_map/ppermute | solution.py:15
  60.1 7.1 %collective-permute-start.5 = (bf16[72,256]{1,0:T(8,128)(2,1)S(1)}, bf16[72,256]{1,0:T(8,128)(2,1)S(1)}, u32[]{:S(2)}, u32[]{:S(2)}) collective-permute-start(bf16[72,256]{1,0:T(8,128)(2,1)S(1)} %collective-permute-done.4), channel_id=1, source_target_pairs={{0,256},{32,288},{64,320},{96,352},{128,384},{160,416},{192,448},{... | collective-permute-start | bytes 110600 | tf_op jit(solution)/shard_map/ppermute | solution.py:15
  68.3 64.8 %all-to-all-start = ((bf16[32,72,256]{2,1,0:T(8,128)(2,1)}), bf16[32,72,256]{2,1,0:T(8,128)(2,1)}, u32[]{:S(2)}, u32[]{:S(2)}) async-start(bf16[32,72,256]{2,1,0:T(8,128)(2,1)} %stack.22), calls=%async_computation | async-start | bytes 2359296 | tf_op jit(solution)/shard_map/all_to_all | solution.py:77
  77.4 364.8 %all-reduce.15.cloned.1.call-start = ((), (), s32[]{:S(2)}) async-start(), calls=%async_computation.2 | async-start | bytes 4718592 | tf_op jit(solution)/shard_map/psum | solution.py:104
  106.8 9.0 %collective-permute-start = (bf16[1,16,16,256]{3,2,1,0:T(8,128)(2,1)S(1)}, bf16[1,16,16,256]{3,2,1,0:T(8,128)(2,1)S(1)}, u32[]{:S(2)}, u32[]{:S(2)}) collective-permute-start(bf16[1,16,16,256]{3,2,1,0:T(8,128)(2,1)S(1)} %bitcast.548), channel_id=1, source_target_pairs={{32,0},{64,32},{96,64},{128,96},{160,128},{192,160},{224,192},{256... | collective-permute-start | bytes 393224 | tf_op jit(solution)/shard_map/ppermute | solution.py:21
  128.4 7.7 %copy-start.9 = (bf16[1,16,16,256]{3,2,1,0:T(8,128)(2,1)}, bf16[1,16,16,256]{3,2,1,0:T(8,128)(2,1)S(1)}, u32[]{:S(2)}) copy-start(bf16[1,16,16,256]{3,2,1,0:T(8,128)(2,1)S(1)} %fusion.125) | copy-start | bytes 393220
  128.4 9.8 %collective-permute-start.1 = (bf16[1,16,16,256]{3,2,1,0:T(8,128)(2,1)S(1)}, bf16[1,16,16,256]{3,2,1,0:T(8,128)(2,1)S(1)}, u32[]{:S(2)}, u32[]{:S(2)}) collective-permute-start(bf16[1,16,16,256]{3,2,1,0:T(8,128)(2,1)S(1)} %fusion.125), channel_id=1, source_target_pairs={{32,0},{64,32},{96,64},{128,96},{160,128},{192,160},{224,192},{256... | collective-permute-start | bytes 393224 | tf_op jit(solution)/shard_map/ppermute | solution.py:21
  136.1 9.0 %collective-permute-start.6 = (bf16[1,16,16,256]{3,2,1,0:T(8,128)(2,1)S(1)}, bf16[1,16,16,256]{3,2,1,0:T(8,128)(2,1)S(1)}, u32[]{:S(2)}, u32[]{:S(2)}) collective-permute-start(bf16[1,16,16,256]{3,2,1,0:T(8,128)(2,1)S(1)} %bitcast.546), channel_id=1, source_target_pairs={{0,32},{32,64},{64,96},{96,128},{128,160},{160,192},{192,224},{224... | collective-permute-start | bytes 393224 | tf_op jit(solution)/shard_map/ppermute | solution.py:21
  158.0 9.1 %copy-start.14 = (bf16[1,16,16,2304]{3,2,1,0:T(8,128)(2,1)S(1)}, bf16[1,16,16,2304]{3,2,1,0:T(8,128)(2,1)}, u32[]{:S(2)}) copy-start(bf16[1,16,16,2304]{3,2,1,0:T(8,128)(2,1)} %copy-done.13) | copy-start | bytes 3538948
  158.0 9.1 %collective-permute-start.7 = (bf16[1,16,16,256]{3,2,1,0:T(8,128)(2,1)S(1)}, bf16[1,16,16,256]{3,2,1,0:T(8,128)(2,1)S(1)}, u32[]{:S(2)}, u32[]{:S(2)}) collective-permute-start(bf16[1,16,16,256]{3,2,1,0:T(8,128)(2,1)S(1)} %fusion.145), channel_id=1, source_target_pairs={{0,32},{32,64},{64,96},{96,128},{128,160},{160,192},{192,224},{224... | collective-permute-start | bytes 393224 | tf_op jit(solution)/shard_map/ppermute | solution.py:21
  443.0 5.8 %collective-permute-start.8 = (bf16[72,256]{1,0:T(8,128)(2,1)S(1)}, bf16[72,256]{1,0:T(8,128)(2,1)S(1)}, u32[]{:S(2)}, u32[]{:S(2)}) collective-permute-start(bf16[72,256]{1,0:T(8,128)(2,1)S(1)} %convert_convert_fusion), channel_id=1, source_target_pairs={{0,32},{32,0},{64,96},{96,64},{128,160},{160,128},{192,224},{224,1... | collective-permute-start | bytes 110600 | tf_op jit(solution)/shard_map/ppermute | solution.py:15
  448.8 7.8 %collective-permute-start.9 = (bf16[72,256]{1,0:T(8,128)(2,1)S(1)}, bf16[72,256]{1,0:T(8,128)(2,1)S(1)}, u32[]{:S(2)}, u32[]{:S(2)}) collective-permute-start(bf16[72,256]{1,0:T(8,128)(2,1)S(1)} %collective-permute-done.8), channel_id=1, source_target_pairs={{0,64},{32,96},{64,0},{96,32},{128,192},{160,224},{192,128},{224,1... | collective-permute-start | bytes 110600 | tf_op jit(solution)/shard_map/ppermute | solution.py:15
  456.6 12.6 %copy-start.8 = (bf16[1,16,16,256]{3,2,1,0:T(8,128)(2,1)S(1)}, bf16[1,16,16,256]{3,2,1,0:T(8,128)(2,1)}, u32[]{:S(2)}) copy-start(bf16[1,16,16,256]{3,2,1,0:T(8,128)(2,1)} %copy-done.7) | copy-start | bytes 393220
  456.6 16.2 %copy-start.6 = (f32[1,72,256]{2,1,0:T(8,128)S(1)}, f32[1,72,256]{2,1,0:T(8,128)}, u32[]{:S(2)}) copy-start(f32[1,72,256]{2,1,0:T(8,128)} %param.11) | copy-start | bytes 221188
  456.7 16.2 %copy-start.11 = (f32[1,72,256]{2,1,0:T(8,128)S(1)}, f32[1,72,256]{2,1,0:T(8,128)}, u32[]{:S(2)}) copy-start(f32[1,72,256]{2,1,0:T(8,128)} %param.13) | copy-start | bytes 221188
  456.7 16.2 %copy-start.12 = (f32[1,72,256]{2,1,0:T(8,128)S(1)}, f32[1,72,256]{2,1,0:T(8,128)}, u32[]{:S(2)}) copy-start(f32[1,72,256]{2,1,0:T(8,128)} %param.12) | copy-start | bytes 221188
  456.7 10.3 %collective-permute-start.10 = (bf16[72,256]{1,0:T(8,128)(2,1)S(1)}, bf16[72,256]{1,0:T(8,128)(2,1)S(1)}, u32[]{:S(2)}, u32[]{:S(2)}) collective-permute-start(bf16[72,256]{1,0:T(8,128)(2,1)S(1)} %collective-permute-done.9), channel_id=1, source_target_pairs={{0,128},{32,160},{64,192},{96,224},{128,0},{160,32},{192,64},{224,... | collective-permute-start | bytes 110600 | tf_op jit(solution)/shard_map/ppermute | solution.py:15
  467.0 5.8 %collective-permute-start.11 = (bf16[72,256]{1,0:T(8,128)(2,1)S(1)}, bf16[72,256]{1,0:T(8,128)(2,1)S(1)}, u32[]{:S(2)}, u32[]{:S(2)}) collective-permute-start(bf16[72,256]{1,0:T(8,128)(2,1)S(1)} %collective-permute-done.10), channel_id=1, source_target_pairs={{0,256},{32,288},{64,320},{96,352},{128,384},{160,416},{192,448},{... | collective-permute-start | bytes 110600 | tf_op jit(solution)/shard_map/ppermute | solution.py:15
  (8 other events, 30.5 us)
Sparse Core Ops, SparseCore 0:
  11.8 92.0 all-gather.1
  170.7 271.4 all-reduce.14
